TPU v7x, 512 devices: a whole 4x4x16 slice. The times are simulated.
512 devices in a mesh: grp: 16 (over z), dev: 32 (over y, x, core).
Axes of the slice: x: 4, y: 4, z: 16, core: 2. Of those that a mesh axis runs over, the one named last changes fastest.
Arguments:
- particles: bfloat16 [8192, 2, 6144], P(('grp', 'dev')), may hold values from -24 to 24
- defocus_bin: int32 [8192], P(('grp', 'dev')), may hold values from 0 to 15
- candidates: int32 [8192, 8], P(('grp', 'dev')), may hold values from 0 to 63, as said below
- projections: bfloat16 [64, 2, 6144], P('dev'), may hold values from -1 to 1
- ctf_table: bfloat16 [16, 6144], replicated, may hold values from -1 to 1
- inv_noise: float32 [6144], replicated, may hold values from 0.25 to 4
- line_slab: int32 [64, 48], P('dev'), may hold values from 0 to 15, as said below
- slab_owner: int32 [16], replicated, may hold values from 0 to 15, each once
Outputs:
- slab_data: float32 [16, 64, 2, 6, 128], P('grp', 'dev')
- slab_weight: float32 [16, 64, 6, 128], P('grp', 'dev')
Inputs may be any that keep to these rules, and one draw needn't show every extreme that they name: `candidates`: each particle lists 8 different projections. `line_slab`: no slab holds more than 6 lines of one projection, and for every projection one slab holds exactly 6 of them. `slab_owner`: each group owns exactly one slab.
All inputs are finite; a program needn't handle non-finite values.
Results may differ from a plain program's by a relative error of at most 0.02.
Values may be sent and summed in bfloat16 or wider, within the bound.
A program may use at most 64 MiB of HBM per device.

v0:
```python
import math
import jax
import jax.numpy as jnp
from jax import lax
from jax.sharding import PartitionSpec as P

LINE_LEN = 128
PIXELS = 6144
SHIFTS = 9
two_pi = 2.0 * math.pi
exact = lax.Precision.HIGHEST
contract_rows = (((0,), (0,)), ((), ()))
contract_last = (((1,), (1,)), ((), ()))


def phase_tables():
    pixel_index = jnp.arange(PIXELS, dtype=jnp.int32)
    line_pos = (pixel_index // LINE_LEN).astype(jnp.float32)
    column = pixel_index % LINE_LEN
    frequency = jnp.where(column < LINE_LEN // 2, column, column - LINE_LEN).astype(jnp.float32)
    shift_index = jnp.arange(SHIFTS, dtype=jnp.int32)
    move_x = (shift_index // 3 - 1).astype(jnp.float32)
    move_y = (shift_index % 3 - 1).astype(jnp.float32)
    angles = (move_x[:, None] * line_pos[None, :] + move_y[:, None] * frequency[None, :]) * (
        two_pi / LINE_LEN
    )
    return (jnp.cos(angles), jnp.sin(angles))


def slot_tables(line_slab, slab_owner, groups):
    group_ids = jnp.arange(groups, dtype=jnp.int32)
    slab_hit = line_slab[:, :, None] == group_ids[None, None, :]
    owner_line = jnp.sum(jnp.where(slab_hit, slab_owner[None, None, :], 0), axis=2)
    line_ids = jnp.arange(line_slab.shape[1], dtype=jnp.int32)
    earlier = line_ids[None, :] < line_ids[:, None]
    same_owner = owner_line[:, :, None] == owner_line[:, None, :]
    line_rank = jnp.sum(jnp.logical_and(same_owner, earlier[None]), axis=2)
    return (owner_line, line_rank)


def route_lines(values, owner_line, line_rank, groups, capacity):
    group_ids = jnp.arange(groups, dtype=jnp.int32)
    slot_ids = jnp.arange(capacity, dtype=jnp.int32)
    selector = jnp.logical_and(
        owner_line[:, None, None, :] == group_ids[None, :, None, None],
        line_rank[:, None, None, :] == slot_ids[None, None, :, None],
    ).astype(jnp.float32)
    packed = jnp.einsum("jocl,jxlp->ojxcp", selector, values, precision=exact)
    return lax.psum_scatter(
        packed.astype(jnp.bfloat16), "grp", scatter_dimension=0, tiled=True
    ).astype(jnp.float32)[0]


def body(
    particles, defocus_bin, candidates, projections, ctf_table, inv_noise, line_slab, slab_owner
):
    part_dev = particles.shape[0]
    pixels = particles.shape[2]
    proj_dev = projections.shape[0]
    groups = lax.axis_size("grp")
    members = lax.axis_size("dev")
    proj_all = proj_dev * members
    line_count = line_slab.shape[1]
    line_len = pixels // line_count
    capacity = 2 * line_count // groups
    cosines, sine_table = phase_tables()
    table_values = ctf_table.astype(jnp.float32)
    ctf_square = table_values * table_values
    noisy_square = ctf_square * inv_noise[None, :]
    onehot = (
        defocus_bin[:, None] == jnp.arange(ctf_table.shape[0], dtype=jnp.int32)[None, :]
    ).astype(jnp.float32)
    ctf_rows = jnp.dot(onehot, table_values, precision=exact)
    weighted = (
        ((inv_noise[None, :] * ctf_rows)[:, None, :] * particles)
        .astype(jnp.bfloat16)
        .reshape(part_dev, 2 * pixels)
    )
    ctf_image = (
        (ctf_rows[:, None, :] * particles).astype(jnp.bfloat16).reshape(part_dev, 2 * pixels)
    )
    values = lax.all_gather(projections, "dev", axis=0, tiled=True).astype(jnp.float32)
    pix_power = values[:, 0] * values[:, 0] + values[:, 1] * values[:, 1]
    bin_power = lax.dot_general(noisy_square, pix_power, contract_last, precision=exact)
    quad_term = jnp.dot(onehot, bin_power, precision=exact)

    def one_shift(tables):
        cos_row, sin_row = tables
        real_part = values[:, 0] * cos_row[None, :] - values[:, 1] * sin_row[None, :]
        imag_part = values[:, 0] * sin_row[None, :] + values[:, 1] * cos_row[None, :]
        rotated = jnp.concatenate([real_part, imag_part], axis=1).astype(jnp.bfloat16)
        return lax.dot_general(weighted, rotated, contract_last, preferred_element_type=jnp.float32)

    scored = lax.map(one_shift, (cosines, sine_table))
    scores = jnp.transpose(scored, (1, 0, 2)) - 0.5 * quad_term[:, None, :]
    proj_ids = jnp.arange(proj_all, dtype=jnp.int32)
    listed = jnp.any(candidates[:, :, None] == proj_ids[None, None, :], axis=1)
    masked = jnp.where(listed[:, None, :], scores, -jnp.inf)
    row_peak = jnp.max(masked, axis=(1, 2), keepdims=True)
    exp_terms = jnp.exp(masked - row_peak)
    posterior = exp_terms / jnp.sum(exp_terms, axis=(1, 2), keepdims=True)
    by_shift = jnp.transpose(posterior.astype(jnp.bfloat16), (1, 0, 2))

    def add_shift(running, inputs):
        weights_now, cos_row, sin_row = inputs
        summed = lax.dot_general(
            weights_now, ctf_image, contract_rows, preferred_element_type=jnp.float32
        )
        real_sum = summed[:, :pixels]
        imag_sum = summed[:, pixels:]
        turned = jnp.stack(
            [
                real_sum * cos_row[None, :] + imag_sum * sin_row[None, :],
                imag_sum * cos_row[None, :] - real_sum * sin_row[None, :],
            ],
            axis=1,
        )
        return (running + turned, None)

    start_sum = jnp.zeros((proj_dev * lax.axis_size("dev"), 2, pixels), jnp.float32)
    result, _ = lax.scan(add_shift, start_sum, (by_shift, cosines, sine_table))
    data_part = lax.psum_scatter(
        result.astype(jnp.bfloat16), "dev", scatter_dimension=0, tiled=True
    ).astype(jnp.float32)
    proj_share = jnp.sum(posterior, axis=1)
    weight_scale = proj_all / (part_dev * groups * members)
    owner_line, line_rank = slot_tables(line_slab, slab_owner, groups)
    data_lines = data_part.reshape(proj_dev, 2, line_count, line_len)
    ctf_rows_sq = ctf_rows * ctf_rows
    weight_part = (
        lax.psum_scatter(
            lax.dot_general(
                proj_share,
                ctf_rows_sq,
                contract_rows,
                precision=exact,
                preferred_element_type=jnp.float32,
            ).astype(jnp.bfloat16),
            "dev",
            scatter_dimension=0,
            tiled=True,
        ).astype(jnp.float32)
        * weight_scale
    )
    stacked = jnp.concatenate(
        [data_lines, weight_part.reshape(proj_dev, 1, line_count, line_len)], axis=1
    )
    routed = route_lines(stacked, owner_line, line_rank, groups, capacity)
    return (routed[None, :, :2], routed[None, :, 2])


def solution(mesh):
    return jax.shard_map(
        body,
        mesh=mesh,
        in_specs=(
            P(("grp", "dev"), None, None),
            P(("grp", "dev")),
            P(("grp", "dev"), None),
            P("dev", None, None),
            P(),
            P(),
            P("dev", None),
            P(),
        ),
        out_specs=(P("grp", "dev", None, None, None), P("grp", "dev", None, None)),
        check_vma=False,
    )
```

profile of v0, /device:TPU:2, one launch (start us, length us, event | category | flops | bytes accessed | tf_op | source)
XLA Modules:
  0.0 495.3 jit_solution(7120821625978491027)
XLA Ops:
  12.2 2.4 fusion.30
  14.6 59.3 %all-gather.2.cloned.1.call-done = bf16[64,2,6144]{2,1,0:T(2,128)(2,1)} async-done(((bf16[2,2,6144]{2,1,0:T(2,128)(2,1)}), bf16[64,2,6144]{2,1,0:T(2,128)(2,1)}) %all-gather.2.cloned.1.call-update) | async-done | bytes 1572880 | tf_op jit(solution)/shard_map/all_gather | solution.py:82
  73.8 3.2 convert_element_type.95
  77.0 3.0 fusion.19
  80.0 59.7 %while.21 = (s32[]{:T(128)}, f32[9,16,64]{2,1,0:T(8,128)}, f32[64,2,6144]{2,1,0:T(2,128)S(1)}, f32[9,6144]{1,0:T(8,128)}, f32[9,6144]{1,0:T(8,128)}, /*index=5*/bf16[16,12288]{1,0:T(8,128)(2,1)}, s32[]{:T(128)}) while((s32[]{:T(128)}, f32[9,16,64]{2,1,0:T(8,128)}, f32[64,2,6144]{2,1,0:T(2,128)S(1)}, f32[9,6144]{1,0:T(8,128)}, ...), condition=%wide.region_2.3_spmd, body=%wide.region_1.2_spmd.sunk | while | flops 31457280 | bytes 17850988 | solution.py:94
  81.1 1.8 copy.56
  94.4 1.8 copy.56
  101.0 1.8 copy.56
  120.9 1.8 copy.56
  139.7 3.1 fusion.20
  146.7 57.7 %while.22 = (s32[]{:T(128)}, f32[64,2,6144]{2,0,1:T(8,128)}, bf16[9,16,64]{2,1,0:T(8,128)(2,1)}, bf16[16,12288]{1,0:T(8,128)(2,1)S(1)}, f32[9,6144]{1,0:T(8,128)}, /*index=5*/f32[9,6144]{1,0:T(8,128)}, s32[]{:T(128)}, s32[]{:T(128)}) while((s32[]{:T(128)}, f32[64,2,6144]{2,0,1:T(8,128)}, bf16[9,16,64]{2,1,0:T(8,128)(2,1)}, ...), condition=%wide.region_6.7_spmd.clone, body=%wide.region_5.6_spmd.clone.sunk | while | flops 29884416 | bytes 19419748 | solution.py:121
  149.5 2.0 maximum_add_fusion.2
  154.2 3.9 maximum_add_fusion.2
  160.9 3.9 maximum_add_fusion.2
  167.5 3.9 maximum_add_fusion.2
  174.1 3.9 maximum_add_fusion.2
  180.7 3.9 maximum_add_fusion.2
  187.4 3.9 maximum_add_fusion.2
  194.0 3.9 maximum_add_fusion.2
  200.6 3.9 maximum_add_fusion.2
  204.5 3.3 convert_element_type.105
  207.8 2.3 convolution_convert_fusion
  212.5 135.4 %all-reduce.9.cloned.1.call-done = (bf16[64,6144]{1,0:T(8,128)(2,1)}, bf16[64,2,6144]{2,0,1:T(8,128)(2,1)}) async-done(((bf16[64,6144]{1,0:T(8,128)(2,1)}, bf16[64,2,6144]{2,0,1:T(8,128)(2,1)}), (bf16[64,6144]{1,0:T(8,128)(2,1)}, bf16[64,2,6144]{2,0,1:T(8,128)(2,1)})) %all-reduce.9.cloned.1.call-update) | async-done | bytes 2359312
  352.2 134.0 %all-reduce.7.cloned.1.call-done = bf16[16,2,3,6,128]{4,1,3,2,0:T(2,128)(2,1)} async-done(((bf16[16,2,3,6,128]{4,1,3,2,0:T(2,128)(2,1)}), bf16[16,2,3,6,128]{4,1,3,2,0:T(2,128)(2,1)}) %all-reduce.7.cloned.1.call-update) | async-done | bytes 147472
  (138 shorter events, 94.2 us)
Async XLA Ops:
  7.2 66.7 %all-gather.2.cloned.1.call-start = ((), (), s32[]{:S(2)}) async-start(), calls=%async_computation | async-start | bytes 1622016 | tf_op jit(solution)/shard_map/all_gather | solution.py:82
  7.9 340.0 %all-reduce.9.cloned.1.call-start = ((), (), s32[]{:S(2)}) async-start(), calls=%async_computation.2 | async-start | bytes 4718592
  9.2 2.8 copy-start
  9.2 2.7 copy-start.4
  84.6 1.0 copy-start.2
  91.2 1.0 copy-start.2
  97.8 1.0 copy-start.2
  104.5 1.0 copy-start.2
  111.1 1.0 copy-start.2
  117.7 1.0 copy-start.2
  124.4 1.0 copy-start.2
  131.0 1.0 copy-start.2
  137.6 1.0 copy-start.2
  139.7 3.1 copy-start.6
  204.5 3.3 copy-start.3
  204.5 3.3 copy-start.1
  207.8 4.4 copy-start.5
  207.8 4.4 copy-start.7
  210.1 276.1 %all-reduce.7.cloned.1.call-start = ((), (), s32[]{:S(2)}) async-start(), calls=%async_computation.1 | async-start | bytes 294912
Sparse Core Ops, SparseCore 0:
  11.1 62.6 all-gather.1
  210.3 137.5 all-reduce.8
  351.1 135.1 all-reduce.6
where the time goes:
time: 497 us; the launch traced here: 495 us
  waiting for transfers between devices  329 us (66%)
  other arithmetic  63.9 us (13%)
  local copies, waits for them, and re-layouts  58.4 us (12%)
  matrix products  28.5 us (6%)
  between operations  14.6 us (3%)
    unnamed x5, waiting for transfers between devices  270 us
    all_gather x1, waiting for transfers between devices, body(): lax.all_gather(projections, 'dev', axis=0, tiled=True).astype(jnp.float32)  59.3 us
    add x9, other arithmetic, add_shift(): return (running + turned, None)  32.9 us
    dynamic_slice x18, local copies, waits for them, and re-layouts, body(): scored = lax.map(one_shift, (cosines, sine_table))  19 us
    another operation x9, local copies, waits for them, and re-layouts  16.4 us
    slice x9, local copies, waits for them, and re-layouts, one_shift(): values[:, 1] * sin_row[None, :]  14.6 us
    dot_general x9, matrix products, add_shift(): lax.dot_general(weights_now, ctf_image, contract_rows, preferred_element_...  11.4 us
    dot_general x9, matrix products, one_shift(): lax.dot_general(weighted, rotated, contract_last, preferred_element_type=...  10.1 us
  transfers between devices with their start and end apart: 3, of which 3 were waited for; matrix products, arithmetic and copies ran while one was open for 2% of the time, Pallas kernels for 0%

commit v1 on v0

--- a/solution.py
+++ b/solution.py
@@ -54,6 +54,13 @@
 def body(
     particles, defocus_bin, candidates, projections, ctf_table, inv_noise, line_slab, slab_owner
 ):
+
+    def edit_entries(vals):
+        return jnp.concatenate(
+            lax.all_to_all(jnp.stack([vals for _ in range(lax.axis_size("dev"))]), "dev", 0, 0),
+            axis=0,
+        )
+
     part_dev = particles.shape[0]
     pixels = particles.shape[2]
     proj_dev = projections.shape[0]
@@ -79,7 +86,7 @@
     ctf_image = (
         (ctf_rows[:, None, :] * particles).astype(jnp.bfloat16).reshape(part_dev, 2 * pixels)
     )
-    values = lax.all_gather(projections, "dev", axis=0, tiled=True).astype(jnp.float32)
+    values = edit_entries(projections).astype(jnp.float32)
     pix_power = values[:, 0] * values[:, 0] + values[:, 1] * values[:, 1]
     bin_power = lax.dot_general(noisy_square, pix_power, contract_last, precision=exact)
     quad_term = jnp.dot(onehot, bin_power, precision=exact)

time: 497 us -> 466 us (0.938)
  waiting for transfers between devices: 329 us -> 285 us
  starting transfers between devices: 0.12 us -> 10.4 us
    all_gather x1 -> x0, waiting for transfers between devices: 59.3 us -> none  [body(): lax.all_gather(projections, 'dev', axis=0, tiled=True).astype(jnp.float32)]
    all_to_all x0 -> x1, waiting for transfers between devices: none -> 16.7 us  [edit_entries(): lax.all_to_all(jnp.stack([vals for _ in range(lax.axis_size('dev'))]), 'd...]
    all_to_all x0 -> x1, starting transfers between devices: none -> 10.3 us  [edit_entries(): lax.all_to_all(jnp.stack([vals for _ in range(lax.axis_size('dev'))]), 'd...]
    another operation x9 -> x10, local copies, waits for them, and re-layouts: 16.4 us -> 19.8 us
    unnamed x5 -> x4, waiting for transfers between devices: 270 us -> 269 us
where the time goes in v1:
time: 466 us; the launch traced here: 464 us
  waiting for transfers between devices  285 us (61%)
  other arithmetic  62.9 us (13%)
  local copies, waits for them, and re-layouts  62.5 us (13%)
  matrix products  27.5 us (6%)
  between operations  14.9 us (3%)
  starting transfers between devices  10.4 us (2%)
    unnamed x4, waiting for transfers between devices  269 us
    add x9, other arithmetic, add_shift(): return (running + turned, None)  32.8 us
    dynamic_slice x18, local copies, waits for them, and re-layouts, body(): scored = lax.map(one_shift, (cosines, sine_table))  19 us
    all_to_all x1, waiting for transfers between devices, edit_entries(): lax.all_to_all(jnp.stack([vals for _ in range(lax.axis_size('dev'))]), 'd...  16.7 us
    another operation x9, local copies, waits for them, and re-layouts  16.4 us
    slice x9, local copies, waits for them, and re-layouts, one_shift(): values[:, 1] * sin_row[None, :]  14.6 us
    dot_general x9, matrix products, add_shift(): lax.dot_general(weights_now, ctf_image, contract_rows, preferred_element_...  11.4 us
    all_to_all x1, starting transfers between devices, edit_entries(): lax.all_to_all(jnp.stack([vals for _ in range(lax.axis_size('dev'))]), 'd...  10.3 us
  transfers between devices with their start and end apart: 3, of which 3 were waited for; matrix products, arithmetic and copies ran while one was open for 2% of the time, Pallas kernels for 0%

profile of v1, /device:TPU:2, one launch (start us, length us, event | category | flops | bytes accessed | tf_op | source)
XLA Modules:
  0.0 464.0 jit_solution(4436556927493014938)
XLA Ops:
  7.2 3.4 stack.8
  10.6 10.3 %all-to-all-start = ((bf16[32,2,2,6144]{3,2,1,0:T(2,128)(2,1)}), bf16[32,2,2,6144]{3,2,1,0:T(2,128)(2,1)}, u32[]{:S(2)}, u32[]{:S(2)}) async-start(bf16[32,2,2,6144]{3,2,1,0:T(2,128)(2,1)} %stack.8), calls=%async_computation | async-start | bytes 3145728 | tf_op jit(solution)/shard_map/all_to_all | solution.py:60
  23.9 2.5 fusion.30
  26.4 16.7 %all-to-all-done = bf16[32,2,2,6144]{3,2,1,0:T(2,128)(2,1)} async-done(((bf16[32,2,2,6144]{3,2,1,0:T(2,128)(2,1)}), bf16[32,2,2,6144]{3,2,1,0:T(2,128)(2,1)}, u32[]{:S(2)}, u32[]{:S(2)}) %all-to-all-start) | async-done | bytes 1572896 | tf_op jit(solution)/shard_map/all_to_all | solution.py:60
  43.1 3.2 bitcast_convert_fusion
  46.3 3.0 fusion.19
  49.3 59.7 %while.21 = (s32[]{:T(128)}, f32[9,16,64]{2,1,0:T(8,128)}, f32[64,2,6144]{2,1,0:T(2,128)S(1)}, f32[9,6144]{1,0:T(8,128)}, f32[9,6144]{1,0:T(8,128)}, /*index=5*/bf16[16,12288]{1,0:T(8,128)(2,1)}, s32[]{:T(128)}) while((s32[]{:T(128)}, f32[9,16,64]{2,1,0:T(8,128)}, f32[64,2,6144]{2,1,0:T(2,128)S(1)}, f32[9,6144]{1,0:T(8,128)}, ...), condition=%wide.region_2.3_spmd, body=%wide.region_1.2_spmd.sunk | while | flops 31457280 | bytes 17850988 | solution.py:101
  50.4 1.8 copy.56
  57.0 1.8 copy.56
  109.0 3.1 fusion.20
  116.0 57.6 %while.22 = (s32[]{:T(128)}, f32[64,2,6144]{2,0,1:T(8,128)}, bf16[9,16,64]{2,1,0:T(8,128)(2,1)}, bf16[16,12288]{1,0:T(8,128)(2,1)S(1)}, f32[9,6144]{1,0:T(8,128)}, /*index=5*/f32[9,6144]{1,0:T(8,128)}, s32[]{:T(128)}, s32[]{:T(128)}) while((s32[]{:T(128)}, f32[64,2,6144]{2,0,1:T(8,128)}, bf16[9,16,64]{2,1,0:T(8,128)(2,1)}, ...), condition=%wide.region_6.7_spmd.clone, body=%wide.region_5.6_spmd.clone.sunk | while | flops 29884416 | bytes 19419748 | solution.py:128
  118.8 2.0 maximum_add_fusion.2
  123.5 3.9 maximum_add_fusion.2
  130.1 3.9 maximum_add_fusion.2
  136.8 3.9 maximum_add_fusion.2
  143.4 3.9 maximum_add_fusion.2
  150.0 3.9 maximum_add_fusion.2
  156.6 3.9 maximum_add_fusion.2
  163.2 3.9 maximum_add_fusion.2
  169.8 3.9 maximum_add_fusion.2
  173.7 3.3 convert_element_type.109
  177.0 2.3 convolution_convert_fusion
  181.6 134.6 %all-reduce.9.cloned.1.call-done = (bf16[64,6144]{1,0:T(8,128)(2,1)}, bf16[64,2,6144]{2,0,1:T(8,128)(2,1)}) async-done(((bf16[64,6144]{1,0:T(8,128)(2,1)}, bf16[64,2,6144]{2,0,1:T(8,128)(2,1)}), (bf16[64,6144]{1,0:T(8,128)(2,1)}, bf16[64,2,6144]{2,0,1:T(8,128)(2,1)})) %all-reduce.9.cloned.1.call-update) | async-done | bytes 2359312
  320.6 134.0 %all-reduce.7.cloned.1.call-done = bf16[16,2,3,6,128]{4,1,3,2,0:T(2,128)(2,1)} async-done(((bf16[16,2,3,6,128]{4,1,3,2,0:T(2,128)(2,1)}), bf16[16,2,3,6,128]{4,1,3,2,0:T(2,128)(2,1)}) %all-reduce.7.cloned.1.call-update) | async-done | bytes 147472
  (144 shorter events, 95.8 us)
Async XLA Ops:
  10.5 10.4 %copy-start.2 = (bf16[16,6144]{1,0:T(8,128)(2,1)S(1)}, bf16[16,6144]{1,0:T(8,128)(2,1)}, u32[]{:S(2)}) copy-start(bf16[16,6144]{1,0:T(8,128)(2,1)} %param.16) | copy-start | bytes 589828
  10.5 10.4 %copy-start.6 = (f32[6144]{0:T(1024)S(1)}, f32[6144]{0:T(1024)}, u32[]{:S(2)}) copy-start(f32[6144]{0:T(1024)} %param.17) | copy-start | bytes 73732
  10.5 10.4 %copy-start.9 = (s32[16]{0:T(128)S(1)}, s32[16]{0:T(128)}, u32[]{:S(2)}) copy-start(s32[16]{0:T(128)} %param.13) | copy-start | bytes 196
  10.5 11.5 %copy-start.4 = (bf16[16,2,6144]{2,1,0:T(2,128)(2,1)S(1)}, bf16[16,2,6144]{2,1,0:T(2,128)(2,1)}, u32[]{:S(2)}) copy-start(bf16[16,2,6144]{2,1,0:T(2,128)(2,1)} %param.12) | copy-start | bytes 1179652
  10.6 32.6 %all-to-all-start = ((bf16[32,2,2,6144]{3,2,1,0:T(2,128)(2,1)}), bf16[32,2,2,6144]{3,2,1,0:T(2,128)(2,1)}, u32[]{:S(2)}, u32[]{:S(2)}) async-start(bf16[32,2,2,6144]{3,2,1,0:T(2,128)(2,1)} %stack.8), calls=%async_computation | async-start | bytes 3145728 | tf_op jit(solution)/shard_map/all_to_all | solution.py:60
  20.9 295.3 %all-reduce.9.cloned.1.call-start = ((), (), s32[]{:S(2)}) async-start(), calls=%async_computation.2 | async-start | bytes 4718592
  21.3 0.8 copy-start
  21.3 2.3 copy-start.7
  53.9 1.0 copy-start.3
  60.5 1.0 copy-start.3
  67.1 1.0 copy-start.3
  73.8 1.0 copy-start.3
  80.4 1.0 copy-start.3
  87.0 1.0 copy-start.3
  93.7 1.0 copy-start.3
  100.3 1.0 copy-start.3
  106.9 1.0 copy-start.3
  173.7 3.3 copy-start.5
  173.7 3.3 copy-start.1
  177.0 4.4 copy-start.8
  177.0 4.3 copy-start.10
  179.3 275.2 %all-reduce.7.cloned.1.call-start = ((), (), s32[]{:S(2)}) async-start(), calls=%async_computation.1 | async-start | bytes 294912
Sparse Core Ops, SparseCore 0:
  179.5 136.7 all-reduce.8
  319.5 135.0 all-reduce.6
